TPU v7x, 256 devices: a whole 4x4x8 slice. The times are simulated.
256 devices in a mesh: group: 32 (over x, y, core), mp: 8 (over z).
Axes of the slice: x: 4, y: 4, z: 8, core: 2. Of those that a mesh axis runs over, the one named last changes fastest.
Arguments:
- hidden: bfloat16 [16384, 1792], P('group')
- norm_gain: float32 [1792], replicated, may hold values from 0.1 to 1.9
- qkv_weight: bfloat16 [1792, 2304], P(None, 'mp'), may hold values from -0.125 to 0.125
- out_weight: bfloat16 [1792, 1792], P('mp'), may hold values from -0.125 to 0.125
- adapter_down: bfloat16 [1792, 1024], P(None, 'mp'), may hold values from -0.125 to 0.125
- adapter_up: bfloat16 [1024, 1792], P('mp'), may hold values from -1.5 to 1.5
- vocab_rows: bfloat16 [4096, 1792], P(('group', 'mp')), may hold values from -0.125 to 0.125
- segments: int32 [16384], P('group'), may hold values from 0 to 127, never falling along the last dimension, each value on 1 to 512 neighbouring positions
- request_adapter: int32 [128], replicated, may hold values from 0 to 63
- adapter_slot: int32 [64], replicated, may hold values from 0 to 63, each once
- page_table: int32 [2048], replicated, may hold values from 0 to 2047, as said below
Outputs:
- layer_update: bfloat16 [16384, 1792], P('group', 'mp')
- state_norms: float32 [16, 16384], P('mp', 'group')
- max_logits: float32 [16384], P(('group', 'mp'))
Inputs may be any that keep to these rules, and one draw needn't show every extreme that they name: A permutation of all pages. Logical page k of group g (entry g * 64 + k) lies in group page_table[g * 64 + k] // 64, and every group holds exactly two of the logical pages of every group. `segments`: every request's tokens stand together and in order; no request has more than 512 tokens. `adapter_slot`: A permutation.
All inputs are finite; a program needn't handle non-finite values.
Results may differ from a plain program's by a relative error of at most 0.013.
Values may be sent and summed in bfloat16 or wider, within the bound.
A program may use at most 64 MiB of HBM per device.

v0:
```python
import jax
import jax.numpy as jnp
from jax import lax
from jax.sharding import PartitionSpec as P

FEAT = 16
HD = 112
RANK = 16
EPSILON = 1e-05
PRECISE = lax.Precision.HIGHEST


def from_behind(value, axis, by):
    size = lax.axis_size(axis)
    pairs = [(i, i + by) for i in range(size) if 0 <= i + by < size]
    return lax.ppermute(value, axis, pairs)


def rms_normed(values, norm_gain):
    wide = values.astype(jnp.float32)
    meansq = jnp.mean(wide * wide, axis=-1, keepdims=True)
    return (wide * lax.rsqrt(meansq + EPSILON) * norm_gain).astype(jnp.bfloat16)


def features(vectors, feat_width):
    linear_part = vectors / feat_width**0.25
    outer_part = (vectors[..., :, None] * vectors[..., None, :]).reshape(
        vectors.shape[:-1] + (feat_width * feat_width,)
    )
    outer_part = outer_part / (2.0 * feat_width) ** 0.5
    ones_part = jnp.ones(vectors.shape[:-1] + (1,), jnp.float32)
    return jnp.concatenate([ones_part, linear_part, outer_part], axis=-1)


def block_step(state_carry, block_inputs, feat_width):
    states, totals, owner_seg = state_carry
    phi_query, phi_key, query_rows, key_rows, value_rows, seg_ids = block_inputs
    scaling = feat_width ** (-0.5)
    block_len = seg_ids.shape[0]
    position = jnp.arange(block_len, dtype=jnp.int32)
    allowed = (
        (position[:, None] >= position[None, :]) & (seg_ids[:, None] == seg_ids[None, :])
    ).astype(jnp.float32)
    carried = (seg_ids == owner_seg).astype(jnp.float32)[None, :]
    scores = jnp.einsum("hcf,hdf->hcd", query_rows, key_rows, precision=PRECISE) * scaling
    weights = (1.0 + scores + 0.5 * scores * scores) * allowed[None]
    numerator = jnp.einsum("hcd,hde->hce", weights, value_rows, precision=PRECISE)
    numerator = numerator + carried[..., None] * jnp.einsum(
        "hcp,hpe->hce", phi_query, states, precision=PRECISE
    )
    denominator = jnp.sum(weights, axis=-1) + carried * jnp.einsum(
        "hcp,hp->hc", phi_query, totals, precision=PRECISE
    )
    mixed_out = numerator / denominator[..., None]
    key_scores = jnp.einsum("hcf,hdf->hcd", key_rows, key_rows, precision=PRECISE) * scaling
    value_gram = jnp.einsum("hce,hde->hcd", value_rows, value_rows, precision=PRECISE)
    key_gram = (1.0 + key_scores + 0.5 * key_scores * key_scores) * value_gram
    masked_gram = jnp.einsum("cd,hde->hce", allowed, key_gram, precision=PRECISE)
    local_squares = jnp.sum(masked_gram * allowed[None], axis=-1)
    along = jnp.sum(
        jnp.einsum("hcp,hpe->hce", phi_key, states, precision=PRECISE) * value_rows, axis=-1
    )
    cross_squares = jnp.einsum("cd,hd->hc", allowed, along, precision=PRECISE)
    state_squares = jnp.sum(states * states, axis=(1, 2))
    squares = carried * (state_squares[:, None] + 2.0 * cross_squares) + local_squares
    counted = carried * totals[:, :1] + jnp.sum(allowed, axis=-1)[None, :]
    state_norm = jnp.sqrt(squares / (counted * (feat_width * value_rows.shape[-1])))
    last_seg = seg_ids[-1]
    member = (seg_ids == last_seg).astype(jnp.float32)
    continues = (owner_seg == last_seg).astype(jnp.float32)
    new_states = continues * states + jnp.einsum(
        "hcp,hce->hpe", phi_key * member[None, :, None], value_rows, precision=PRECISE
    )
    new_totals = continues * totals + jnp.einsum("hcp,c->hp", phi_key, member, precision=PRECISE)
    return ((new_states, new_totals, last_seg), (mixed_out, state_norm))


def best_of(candidates, piece):
    logits = jnp.einsum("rd,vd->rv", candidates, piece, preferred_element_type=jnp.float32)
    return jnp.max(logits, axis=1)


def on_device(
    hidden,
    norm_gain,
    qkv_weight,
    out_weight,
    adapter_down,
    adapter_up,
    vocab_rows,
    segments,
    request_adapter,
    adapter_slot,
    page_table,
):
    groups = lax.axis_size("group")
    own_group = lax.axis_index("group")
    shards = lax.axis_size("mp")
    own_shard = lax.axis_index("mp")
    rows_here = segments.shape[0]
    model_width = hidden.shape[1]
    slice_width = model_width // shards
    table = page_table.reshape(groups, -1)
    per_group = table.shape[1]
    per_peer = per_group // groups
    page_len = rows_here // per_group
    holders = table // per_group
    position = jnp.arange(per_group, dtype=jnp.int32)
    sort_keys = jnp.where(holders == own_group, position[None, :], per_group + position[None, :])
    ranked = jnp.argsort(sort_keys, axis=1)[:, :per_peer]
    picked = jnp.take_along_axis(table, ranked, axis=1) - own_group * per_group
    outgoing = hidden.reshape(per_group, page_len, model_width)[picked]
    normed_pages = rms_normed(outgoing, norm_gain)
    projected_pages = jnp.einsum(
        "abrd,dc->abrc", normed_pages, qkv_weight, preferred_element_type=jnp.float32
    ).astype(jnp.bfloat16)
    lowered_pages = jnp.einsum(
        "abrd,dc->abrc", normed_pages, adapter_down, preferred_element_type=jnp.float32
    ).astype(jnp.bfloat16)
    kept_pages = lax.dynamic_slice_in_dim(outgoing, own_shard * slice_width, slice_width, 3)
    arrived = (
        lax.all_to_all(kept_pages, "group", split_axis=0, concat_axis=0, tiled=True),
        lax.all_to_all(projected_pages, "group", split_axis=0, concat_axis=0, tiled=True),
        lax.all_to_all(lowered_pages, "group", split_axis=0, concat_axis=0, tiled=True),
    )
    own_holders = lax.dynamic_index_in_dim(holders, own_group, 0, keepdims=False)
    onehot = (own_holders[:, None] == jnp.arange(groups, dtype=jnp.int32)[None, :]).astype(
        jnp.int32
    )
    earlier = jnp.sum((jnp.cumsum(onehot, axis=0) - onehot) * onehot, axis=1)
    source_rows = own_holders * per_peer + earlier

    def placed(received):
        gathered_rows = received.reshape((groups * per_peer,) + received.shape[2:])[source_rows]
        return gathered_rows.reshape((rows_here,) + received.shape[3:])

    residual, projected, lowered = [placed(received) for received in arrived]
    heads_here = projected.shape[1] // (2 * FEAT + HD)
    split_heads = jnp.transpose(
        projected.reshape(rows_here, heads_here, 2 * FEAT + HD).astype(jnp.float32), (1, 0, 2)
    )
    query_rows = split_heads[..., :FEAT]
    key_rows = split_heads[..., FEAT : 2 * FEAT]
    value_rows = split_heads[..., 2 * FEAT :]
    phi_query = features(query_rows, FEAT)
    phi_key = features(key_rows, FEAT)
    last_seg = segments[-1]
    member = (segments == last_seg).astype(jnp.float32)
    end_state = jnp.einsum(
        "hcp,hce->hpe", phi_key * member[None, :, None], value_rows, precision=PRECISE
    )
    end_totals = jnp.einsum("hcp,c->hp", phi_key, member, precision=PRECISE)
    end_tag = jnp.reshape(last_seg + 1, (1,)).astype(jnp.float32)
    got_state, got_totals, got_tag = (
        from_behind(end_state.astype(jnp.bfloat16), "group", 1).astype(end_state.dtype),
        from_behind(end_totals.astype(jnp.bfloat16), "group", 1).astype(end_totals.dtype),
        from_behind(end_tag.astype(jnp.bfloat16), "group", 1).astype(end_tag.dtype),
    )
    initial = (got_state, got_totals, got_tag[0].astype(jnp.int32) - 1)
    block_len = min(256, rows_here)
    blocks = rows_here // block_len

    def regroup(values):
        return jnp.transpose(
            values.reshape(values.shape[0], blocks, block_len, values.shape[-1]), (1, 0, 2, 3)
        )

    scan_inputs = (
        regroup(phi_query),
        regroup(phi_key),
        regroup(query_rows),
        regroup(key_rows),
        regroup(value_rows),
        segments.reshape(blocks, block_len),
    )

    def scan_step(state_carry, block_inputs):
        return block_step(state_carry, block_inputs, FEAT)

    _, (mixed_out, state_norm) = lax.scan(scan_step, initial, scan_inputs)
    attended = (
        jnp.transpose(mixed_out, (0, 2, 1, 3))
        .reshape(rows_here, heads_here * HD)
        .astype(jnp.bfloat16)
    )
    state_norms = jnp.transpose(state_norm, (1, 0, 2)).reshape(heads_here, rows_here)
    request_ids = jnp.arange(request_adapter.shape[0], dtype=jnp.int32)
    adapter_of = jnp.sum(
        jnp.where(segments[:, None] == request_ids[None, :], request_adapter[None, :], 0), axis=1
    )
    adapter_ids = jnp.arange(adapter_slot.shape[0], dtype=jnp.int32)
    slot_ids = jnp.sum(
        jnp.where(adapter_of[:, None] == adapter_ids[None, :], adapter_slot[None, :], 0), axis=1
    )
    column_slot = jnp.arange(lowered.shape[1], dtype=jnp.int32) // RANK
    local_slot = slot_ids - own_shard * (lowered.shape[1] // RANK)
    low_rank = jnp.where(
        local_slot[:, None] == column_slot[None, :], lowered, jnp.zeros_like(lowered)
    )
    partial_value = jnp.dot(attended, out_weight, preferred_element_type=jnp.float32)
    partial_value = partial_value + jnp.dot(
        low_rank, adapter_up, preferred_element_type=jnp.float32
    )
    summed = lax.psum_scatter(
        partial_value.astype(jnp.bfloat16), "mp", scatter_dimension=1, tiled=True
    )
    final_rows = (residual.astype(jnp.float32) + summed.astype(jnp.float32)).astype(jnp.bfloat16)
    own_rows = lax.all_to_all(final_rows, "mp", split_axis=0, concat_axis=1, tiled=True)
    max_logits = best_of(own_rows, lax.all_gather(vocab_rows, ("group", "mp"), axis=0, tiled=True))
    return (summed, state_norms, max_logits)


def solution(mesh):
    placed = (
        P("group", None),
        P(),
        P(None, "mp"),
        P("mp", None),
        P(None, "mp"),
        P("mp", None),
        P(("group", "mp"), None),
        P("group"),
        P(),
        P(),
        P(),
    )
    return jax.shard_map(
        on_device,
        mesh=mesh,
        in_specs=placed,
        out_specs=(P("group", "mp"), P("mp", "group"), P(("group", "mp"))),
        check_vma=False,
    )
```

profile of v0, /device:TPU:1, one launch (start us, length us, event | category | flops | bytes accessed | tf_op | source)
XLA Modules:
  0.0 277.1 jit_solution(12786450912121898422)
XLA Ops:
  10.1 5.3 %collective-permute-start.2 = (bf16[1]{0:T(256)(128)(2,1)}, bf16[1]{0:T(256)(128)(2,1)}, u32[]{:S(2)}, u32[]{:S(2)}) collective-permute-start(bf16[1]{0:T(256)(128)(2,1)} %bitcast.30), channel_id=1, source_target_pairs={{0,8},{8,16},{16,24},{24,32},{32,40},{40,48},{48,56},{56,64},{64,7... | collective-permute-start | bytes 14 | tf_op jit(solution)/shard_map/ppermute | solution.py:16
  18.7 1.9 gather_fusion
  20.6 2.0 fusion.49
  22.8 3.0 %fusion.59 = bf16[32,2,8,128]{3,2,1,0:T(8,128)(2,1)} fusion(bf16[32,2,8,1792]{3,2,1,0:T(8,128)(2,1)} %bitcast.226, f32[1792]{0:T(1024)S(1)} %copy-done.19, f32[32,2,8]{2,1,0:T(2,128)S(1)} %copy.95, bf16[1792,128]{1,0:T(8,128)(2,1)} %param.17), kind=kOutput, calls=%fused_computation.84 | convolution fusion | flops 238616576 | bytes 2434048 | tf_op jit(solution)/shard_map/abrd,dc->abrc/dot_general | solution.py:117
  25.8 6.9 %all-to-all-start.1 = ((bf16[32,2,8,128]{3,2,1,0:T(8,128)(2,1)}), bf16[32,2,8,128]{3,2,1,0:T(8,128)(2,1)S(1)}, u32[]{:S(2)}, u32[]{:S(2)}) async-start(bf16[32,2,8,128]{3,2,1,0:T(8,128)(2,1)} %fusion.59), calls=%async_computation.1 | async-start | bytes 262144 | tf_op jit(solution)/shard_map/all_to_all | solution.py:124
  33.4 3.4 %fusion.56 = bf16[32,2,8,288]{3,2,1,0:T(8,128)(2,1)} fusion(bf16[32,2,8,1792]{3,2,1,0:T(8,128)(2,1)} %bitcast.227, f32[1792]{0:T(1024)S(1)} %copy-done.19, f32[32,2,8]{2,1,0:T(2,128)S(1)} %copy.95, bf16[1792,288]{0,1:T(8,128)(2,1)S(1)} %copy-done.18), kind=kOutput, calls=%fused_computation.81 | convolution fusion | flops 532299776 | bytes 3171328 | tf_op jit(solution)/shard_map/abrd,dc->abrc/dot_general | solution.py:114
  38.2 2.2 all-to-all-done.1
  40.4 5.2 %all-to-all-start = ((bf16[32,2,8,288]{3,2,1,0:T(8,128)(2,1)}), bf16[32,2,8,288]{3,2,1,0:T(8,128)(2,1)S(1)}, u32[]{:S(2)}, u32[]{:S(2)}) async-start(bf16[32,2,8,288]{3,2,1,0:T(8,128)(2,1)} %fusion.56), calls=%async_computation | async-start | bytes 786432 | tf_op jit(solution)/shard_map/all_to_all | solution.py:123
  48.8 7.1 %all-to-all-done = bf16[32,2,8,288]{3,2,1,0:T(8,128)(2,1)S(1)} async-done(((bf16[32,2,8,288]{3,2,1,0:T(8,128)(2,1)}), bf16[32,2,8,288]{3,2,1,0:T(8,128)(2,1)S(1)}, u32[]{:S(2)}, u32[]{:S(2)}) %all-to-all-start) | async-done | bytes 294944 | tf_op jit(solution)/shard_map/all_to_all | solution.py:123
  61.0 1.9 collective-permute-start
  64.4 2.6 collective-permute-start.1
  68.5 1.7 reshape.241
  71.7 1.7 reshape.245
  75.2 48.3 %while.21 = (s32[]{:T(128)}, f32[2,273,112]{2,1,0:T(8,128)S(1)}, f32[2,273]{0,1:T(8,128)S(1)}, s32[]{:T(128)}, bf16[2,2,256,112]{2,3,1,0:T(8,128)(2,1)}, /*index...) while((s32[]{:T(128)}, f32[2,273,112]{2,1,0:T(8,128)S(1)}, ...), condition=%wide.region_10.11_spmd, body=%wide.region_4.10_spmd.sunk | while | flops 1377437056 | bytes 16456851 | solution.py:180
  75.9 2.5 constant_dynamic-slice_fusion.7
  78.4 1.5 fusion.142
  83.2 1.6 convolution_multiply_fusion.6
  85.4 1.7 convolution_add_fusion.3
  90.9 1.5 fusion.136
  93.7 2.1 fusion.139
  100.0 2.5 constant_dynamic-slice_fusion.7
  107.3 1.6 convolution_multiply_fusion.6
  109.5 1.7 convolution_add_fusion.3
  115.1 1.5 fusion.136
  117.8 2.1 fusion.139
  124.8 1.9 fusion.81
  126.7 2.0 add_convert_fusion
  130.5 14.5 %all_to_all.34 = bf16[32,2,8,224]{3,2,1,0:T(8,128)(2,1)S(1)} all-to-all(bf16[32,2,8,224]{3,2,1,0:T(8,128)(2,1)S(1)} %constant_dynamic-slice_fusion.3), channel_id=1, replica_groups=mesh['group'=32,'mp'=8] {'group'}, dimensions={0} | all-to-all | bytes 458752 | tf_op jit(solution)/shard_map/all_to_all | solution.py:122
  145.9 21.4 %reduce-scatter.2.cloned.1.call-done = bf16[512,224]{0,1:T(8,128)(2,1)} async-done(((bf16[512,1792]{0,1:T(8,128)(2,1)}), bf16[512,224]{0,1:T(8,128)(2,1)}) %reduce-scatter.2.cloned.1.call-update) | async-done | bytes 229392 | tf_op jit(solution)/shard_map/reduce_scatter | solution.py:204
  168.4 14.1 %all_to_all.35 = bf16[8,64,224]{2,1,0:T(8,128)(2,1)S(1)} all-to-all(bf16[8,64,224]{2,1,0:T(8,128)(2,1)S(1)} %bitcast.244), channel_id=1, replica_groups=mesh['group'=32,'mp'=8] {'mp'}, dimensions={0} | all-to-all | bytes 458752 | tf_op jit(solution)/shard_map/all_to_all | solution.py:208
  183.0 76.4 %all-gather.2.cloned.1.call-done = bf16[4096,1792]{1,0:T(8,128)(2,1)} async-done(((bf16[16,1792]{1,0:T(8,128)(2,1)}), bf16[4096,1792]{1,0:T(8,128)(2,1)}) %all-gather.2.cloned.1.call-update) | async-done | bytes 14680080 | tf_op jit(solution)/shard_map/all_gather | solution.py:209
  259.4 10.3 %convolution_reduce_fusion = f32[64]{0:T(128)} fusion(bf16[64,1792]{1,0:T(8,128)(2,1)S(1)} %all_to_all.29, bf16[4096,1792]{1,0:T(8,128)(2,1)} %all-gather.2.cloned.1.call-done), kind=kOutput, calls=%fused_computation.82 | convolution fusion | flops 939786176 | bytes 14909696 | tf_op jit(solution)/shard_map/rd,vd->rv/dot_general | solution.py:79
  (171 shorter events, 51.1 us)
Async XLA Ops:
  8.0 10.7 %copy-start = (bf16[512,1792]{1,0:T(8,128)(2,1)S(1)}, bf16[512,1792]{1,0:T(8,128)(2,1)}, u32[]{:S(2)}) copy-start(bf16[512,1792]{1,0:T(8,128)(2,1)} %param.13) | copy-start | bytes 5505028
  10.1 36.8 %collective-permute-start.2 = (bf16[1]{0:T(256)(128)(2,1)}, bf16[1]{0:T(256)(128)(2,1)}, u32[]{:S(2)}, u32[]{:S(2)}) collective-permute-start(bf16[1]{0:T(256)(128)(2,1)} %bitcast.30), channel_id=1, source_target_pairs={{0,8},{8,16},{16,24},{24,32},{32,40},{40,48},{48,56},{56,64},{64,7... | collective-permute-start | bytes 14 | tf_op jit(solution)/shard_map/ppermute | solution.py:16
  20.6 2.1 copy-start.19
  22.8 9.9 %copy-start.11 = (s32[512]{0:T(512)S(1)}, s32[512]{0:T(512)}, u32[]{:S(2)}) copy-start(s32[512]{0:T(512)} %param.20) | copy-start | bytes 6148
  22.8 10.6 %copy-start.18 = (bf16[1792,288]{0,1:T(8,128)(2,1)S(1)}, bf16[1792,288]{0,1:T(8,128)(2,1)}, u32[]{:S(2)}) copy-start(bf16[1792,288]{0,1:T(8,128)(2,1)} %param.15) | copy-start | bytes 3096580
  25.8 14.6 %all-to-all-start.1 = ((bf16[32,2,8,128]{3,2,1,0:T(8,128)(2,1)}), bf16[32,2,8,128]{3,2,1,0:T(8,128)(2,1)S(1)}, u32[]{:S(2)}, u32[]{:S(2)}) async-start(bf16[32,2,8,128]{3,2,1,0:T(8,128)(2,1)} %fusion.59), calls=%async_computation.1 | async-start | bytes 262144 | tf_op jit(solution)/shard_map/all_to_all | solution.py:124
  33.4 3.8 %copy-start.16 = (s32[128]{0:T(128)S(1)}, s32[128]{0:T(128)}, u32[]{:S(2)}) copy-start(s32[128]{0:T(128)} %param.21) | copy-start | bytes 1540
  33.4 4.7 %copy-start.17 = (s32[64]{0:T(128)S(1)}, s32[64]{0:T(128)}, u32[]{:S(2)}) copy-start(s32[64]{0:T(128)} %param.22) | copy-start | bytes 772
  37.5 19.8 %copy-start.14 = (s32[1024]{0:T(1024)}, s32[1024]{0:T(1024)S(1)}, u32[]{:S(2)}) copy-start(s32[1024]{0:T(1024)S(1)} %pad_clamp_fusion) | copy-start | bytes 12292
  40.4 15.5 %all-to-all-start = ((bf16[32,2,8,288]{3,2,1,0:T(8,128)(2,1)}), bf16[32,2,8,288]{3,2,1,0:T(8,128)(2,1)S(1)}, u32[]{:S(2)}, u32[]{:S(2)}) async-start(bf16[32,2,8,288]{3,2,1,0:T(8,128)(2,1)} %fusion.56), calls=%async_computation | async-start | bytes 786432 | tf_op jit(solution)/shard_map/all_to_all | solution.py:123
  45.6 121.7 %reduce-scatter.2.cloned.1.call-start = ((), (), s32[]{:S(2)}) async-start(), calls=%async_computation.5 | async-start | bytes 2064384 | tf_op jit(solution)/shard_map/reduce_scatter | solution.py:204
  57.3 2.4 copy-start.5
  61.0 13.3 %collective-permute-start = (bf16[2,273,112]{2,1,0:T(8,128)(2,1)}, bf16[2,273,112]{2,1,0:T(8,128)(2,1)}, u32[]{:S(2)}, u32[]{:S(2)}) collective-permute-start(bf16[2,273,112]{2,1,0:T(8,128)(2,1)} %convolution_convert_fusion), channel_id=1, source_target_pairs={{0,8},{8,16},{16,24},{24,32},{32,40},{40,48},{48,56},{56,64},{64,7... | collective-permute-start | bytes 366920 | tf_op jit(solution)/shard_map/ppermute | solution.py:16
  63.6 6.7 %slice-start = ((f32[2,512,144]{1,2,0:T(8,128)}), f32[2,512,112]{1,2,0:T(8,128)S(1)}, s32[]{:S(2)}) async-start(f32[2,512,144]{1,2,0:T(8,128)} %copy-done.4), calls=%async_computation.7 | async-start | bytes 917504 | tf_op jit(solution)/shard_map/slice | solution.py:144
  64.4 9.0 %collective-permute-start.1 = (bf16[2,273]{0,1:T(8,128)(2,1)}, bf16[2,273]{0,1:T(8,128)(2,1)}, u32[]{:S(2)}, u32[]{:S(2)}) collective-permute-start(bf16[2,273]{0,1:T(8,128)(2,1)} %bitcast.250), channel_id=1, source_target_pairs={{0,8},{8,16},{16,24},{24,32},{32,40},{40,48},{48,56},{56,64},{64,7... | collective-permute-start | bytes 3284 | tf_op jit(solution)/shard_map/ppermute | solution.py:16
  75.2 3.2 %copy-start.1 = (f32[2,2,256,112]{2,3,1,0:T(8,128)S(1)}, f32[2,2,256,112]{2,3,1,0:T(8,128)}, u32[]{:S(2)}) copy-start(f32[2,2,256,112]{2,3,1,0:T(8,128)} %get-tuple-element.408) | copy-start | bytes 1376260 | tf_op jit(solution)/shard_map/while
  88.8 4.8 %copy-start.2 = (f32[2,2,256,112]{2,3,1,0:T(8,128)S(1)}, f32[2,2,256,112]{2,3,1,0:T(8,128)}, u32[]{:S(2)}) copy-start(f32[2,2,256,112]{2,3,1,0:T(8,128)} %get-tuple-element.408) | copy-start | bytes 1376260 | tf_op jit(solution)/shard_map/while
  90.9 4.8 %copy-start.6 = (f32[2,2,256,16]{2,3,1,0:T(8,128)S(1)}, f32[2,2,256,16]{2,3,1,0:T(8,128)}, u32[]{:S(2)}) copy-start(f32[2,2,256,16]{2,3,1,0:T(8,128)} %get-tuple-element.410) | copy-start | bytes 196612 | tf_op jit(solution)/shard_map/while
  93.6 4.1 %copy-start.9 = (f32[1,256]{1,0:T(1,128)S(1)}, f32[1,256]{1,0:T(1,128)}, u32[]{:S(2)}) copy-start(f32[1,256]{1,0:T(1,128)} %get-tuple-element.369) | copy-start | bytes 3076 | tf_op jit(solution)/shard_map/while
  93.6 4.1 %copy-start.10 = (f32[2,256]{1,0:T(2,128)S(1)}, f32[2,256]{1,0:T(2,128)}, u32[]{:S(2)}) copy-start(f32[2,256]{1,0:T(2,128)} %fusion.142) | copy-start | bytes 6148 | tf_op jit(solution)/shard_map/while
  93.6 4.1 %copy-start.12 = (f32[2]{0:T(128)S(1)}, f32[2]{0:T(128)}, u32[]{:S(2)}) copy-start(f32[2]{0:T(128)} %multiply_reduce_fusion.2) | copy-start | bytes 28 | tf_op jit(solution)/shard_map/while
  93.7 4.1 %copy-start.20 = (f32[2,2,256]{2,1,0:T(2,128)S(1)}, f32[2,2,256]{2,1,0:T(2,128)}, u32[]{:S(2)}) copy-start(f32[2,2,256]{2,1,0:T(2,128)} %get-tuple-element.390) | copy-start | bytes 12292 | tf_op jit(solution)/shard_map/while
  93.7 4.1 %copy-start.22 = (f32[2]{0:T(128)S(1)}, f32[2]{0:T(128)}, u32[]{:S(2)}) copy-start(f32[2]{0:T(128)} %slice_bitcast_fusion.2) | copy-start | bytes 28 | tf_op jit(solution)/shard_map/while
  99.4 3.2 %copy-start.1 = (f32[2,2,256,112]{2,3,1,0:T(8,128)S(1)}, f32[2,2,256,112]{2,3,1,0:T(8,128)}, u32[]{:S(2)}) copy-start(f32[2,2,256,112]{2,3,1,0:T(8,128)} %get-tuple-element.408) | copy-start | bytes 1376260 | tf_op jit(solution)/shard_map/while
  113.0 4.8 %copy-start.2 = (f32[2,2,256,112]{2,3,1,0:T(8,128)S(1)}, f32[2,2,256,112]{2,3,1,0:T(8,128)}, u32[]{:S(2)}) copy-start(f32[2,2,256,112]{2,3,1,0:T(8,128)} %get-tuple-element.408) | copy-start | bytes 1376260 | tf_op jit(solution)/shard_map/while
  115.1 4.8 %copy-start.6 = (f32[2,2,256,16]{2,3,1,0:T(8,128)S(1)}, f32[2,2,256,16]{2,3,1,0:T(8,128)}, u32[]{:S(2)}) copy-start(f32[2,2,256,16]{2,3,1,0:T(8,128)} %get-tuple-element.410) | copy-start | bytes 196612 | tf_op jit(solution)/shard_map/while
  117.8 4.1 %copy-start.9 = (f32[1,256]{1,0:T(1,128)S(1)}, f32[1,256]{1,0:T(1,128)}, u32[]{:S(2)}) copy-start(f32[1,256]{1,0:T(1,128)} %get-tuple-element.369) | copy-start | bytes 3076 | tf_op jit(solution)/shard_map/while
  117.8 4.1 %copy-start.10 = (f32[2,256]{1,0:T(2,128)S(1)}, f32[2,256]{1,0:T(2,128)}, u32[]{:S(2)}) copy-start(f32[2,256]{1,0:T(2,128)} %fusion.142) | copy-start | bytes 6148 | tf_op jit(solution)/shard_map/while
  117.8 4.1 %copy-start.12 = (f32[2]{0:T(128)S(1)}, f32[2]{0:T(128)}, u32[]{:S(2)}) copy-start(f32[2]{0:T(128)} %multiply_reduce_fusion.2) | copy-start | bytes 28 | tf_op jit(solution)/shard_map/while
  117.8 4.1 %copy-start.20 = (f32[2,2,256]{2,1,0:T(2,128)S(1)}, f32[2,2,256]{2,1,0:T(2,128)}, u32[]{:S(2)}) copy-start(f32[2,2,256]{2,1,0:T(2,128)} %get-tuple-element.390) | copy-start | bytes 12292 | tf_op jit(solution)/shard_map/while
  117.8 4.1 %copy-start.22 = (f32[2]{0:T(128)S(1)}, f32[2]{0:T(128)}, u32[]{:S(2)}) copy-start(f32[2]{0:T(128)} %slice_bitcast_fusion.2) | copy-start | bytes 28 | tf_op jit(solution)/shard_map/while
  128.8 130.6 %all-gather.2.cloned.1.call-start = ((), (), s32[]{:S(2)}) async-start(), calls=%async_computation.6 | async-start | bytes 14737408 | tf_op jit(solution)/shard_map/all_gather | solution.py:209
  (8 other events, 11.2 us)
Sparse Core Ops, SparseCore 0:
  128.9 38.3 reduce-scatter.1
Sparse Core Ops, SparseCore 1:
  132.8 126.5 all-gather.1
where the time goes:
time: 278 us; the launch traced here: 277 us
  waiting for transfers between devices  108 us (39%)
  matrix products  46.6 us (17%)
  local copies, waits for them, and re-layouts  33.4 us (12%)
  blocking collectives  28.6 us (10%)
  starting transfers between devices  22 us (8%)
  other arithmetic  18.6 us (7%)
  between operations  17.3 us (6%)
  loops' own time  2.95 us (1%)
    all_gather x1, waiting for transfers between devices, on_device(): lax.all_gather(vocab_rows, ('group', 'mp'), axis=0, tiled=True)  76.4 us
    reduce_scatter x1, waiting for transfers between devices, on_device(): lax.psum_scatter(partial_value.astype(jnp.bfloat16), 'mp', scatter_dimens...  21.4 us
    all_to_all x1, blocking collectives, on_device(): lax.all_to_all(kept_pages, 'group', split_axis=0, concat_axis=0, tiled=True)  14.5 us
    all_to_all x1, blocking collectives, on_device(): lax.all_to_all(final_rows, 'mp', split_axis=0, concat_axis=1, tiled=True)  14.1 us
    dot_general x1, matrix products, best_of(): jnp.einsum('rd,vd->rv', candidates, piece, preferred_element_type=jnp.flo...  10.3 us
    ppermute x3, starting transfers between devices, from_behind(): return lax.ppermute(value, axis, pairs)  9.84 us
    all_to_all x1, waiting for transfers between devices, on_device(): lax.all_to_all(projected_pages, 'group', split_axis=0, concat_axis=0, til...  7.1 us
    all_to_all x1, starting transfers between devices, on_device(): lax.all_to_all(lowered_pages, 'group', split_axis=0, concat_axis=0, tiled...  6.91 us
  transfers between devices with their start and end apart: 7, of which 4 were waited for; matrix products, arithmetic and copies ran while one was open for 11% of the time, Pallas kernels for 0%

commit v1 on v0

--- a/solution.py
+++ b/solution.py
@@ -2,6 +2,7 @@
 import jax.numpy as jnp
 from jax import lax
 from jax.sharding import PartitionSpec as P
+from jax.lax import all_to_all, psum
 
 FEAT = 16
 HD = 112
@@ -93,6 +94,13 @@
     adapter_slot,
     page_table,
 ):
+
+    def tracks_advance(u, mesh_dim, ndim_at):
+        small = jnp.concatenate(
+            all_to_all(jnp.stack([u for _ in range(psum(1, mesh_dim))], 0), mesh_dim, 0, 0), ndim_at
+        )
+        return small
+
     groups = lax.axis_size("group")
     own_group = lax.axis_index("group")
     shards = lax.axis_size("mp")
@@ -206,7 +214,7 @@
     )
     final_rows = (residual.astype(jnp.float32) + summed.astype(jnp.float32)).astype(jnp.bfloat16)
     own_rows = lax.all_to_all(final_rows, "mp", split_axis=0, concat_axis=1, tiled=True)
-    max_logits = best_of(own_rows, lax.all_gather(vocab_rows, ("group", "mp"), axis=0, tiled=True))
+    max_logits = best_of(own_rows, tracks_advance(vocab_rows, ("group", "mp"), 0))
     return (summed, state_norms, max_logits)
 
 

time: 278 us -> 515 us (1.85)
  waiting for transfers between devices: 108 us -> 352 us
  starting transfers between devices: 22 us -> 34.9 us
  matrix products: 46.6 us -> 37.3 us
  other arithmetic: 18.6 us -> 11.2 us
    all_to_all x0 -> x1, waiting for transfers between devices: none -> 319 us  [tracks_advance(): all_to_all(jnp.stack([u for _ in range(psum(1, mesh_dim))], 0), mesh_dim,...]
    all_gather x1 -> x0, waiting for transfers between devices: 76.4 us -> none  [on_device(): lax.all_gather(vocab_rows, ('group', 'mp'), axis=0, tiled=True)]
    all_to_all x0 -> x1, starting transfers between devices: none -> 13.4 us  [tracks_advance(): all_to_all(jnp.stack([u for _ in range(psum(1, mesh_dim))], 0), mesh_dim,...]
    another operation x2 -> x3, local copies, waits for them, and re-layouts: 0.17 us -> 6.31 us  [the longest x1 6.14 us: tracks_advance(): jnp.stack([u for _ in range(psum(1, mesh_dim))], 0)]
  transfers between devices with their start and end apart: 7 -> 7, of which waited for: 4 -> 4; matrix products, arithmetic and copies ran while one was open for 11% -> 5% of each run, Pallas kernels for 0% -> 0%
where the time goes in v1:
time: 515 us; the launch traced here: 513 us
  waiting for transfers between devices  352 us (68%)
  matrix products  37.3 us (7%)
  starting transfers between devices  34.9 us (7%)
  local copies, waits for them, and re-layouts  30.2 us (6%)
  blocking collectives  28.5 us (6%)
  between operations  15.8 us (3%)
  other arithmetic  11.2 us (2%)
    all_to_all x1, waiting for transfers between devices, tracks_advance(): all_to_all(jnp.stack([u for _ in range(psum(1, mesh_dim))], 0), mesh_dim,...  319 us
    reduce_scatter x1, waiting for transfers between devices, on_device(): lax.psum_scatter(partial_value.astype(jnp.bfloat16), 'mp', scatter_dimens...  22 us
    all_to_all x1, blocking collectives, on_device(): lax.all_to_all(kept_pages, 'group', split_axis=0, concat_axis=0, tiled=True)  14.5 us
    all_to_all x1, blocking collectives, on_device(): lax.all_to_all(final_rows, 'mp', split_axis=0, concat_axis=1, tiled=True)  14 us
    all_to_all x1, starting transfers between devices, tracks_advance(): all_to_all(jnp.stack([u for _ in range(psum(1, mesh_dim))], 0), mesh_dim,...  13.4 us
  transfers between devices with their start and end apart: 7, of which 4 were waited for; matrix products, arithmetic and copies ran while one was open for 5% of the time, Pallas kernels for 0%

profile of v1, /device:TPU:1, one launch (start us, length us, event | category | flops | bytes accessed | tf_op | source)
XLA Modules:
  0.0 513.0 jit_solution(10938335262686065353)
XLA Ops:
  7.2 1.4 slice.34
  9.2 5.3 %collective-permute-start.2 = (bf16[1]{0:T(256)(128)(2,1)}, bf16[1]{0:T(256)(128)(2,1)}, u32[]{:S(2)}, u32[]{:S(2)}) collective-permute-start(bf16[1]{0:T(256)(128)(2,1)} %bitcast.30), channel_id=1, source_target_pairs={{0,8},{8,16},{16,24},{24,32},{32,40},{40,48},{48,56},{56,64},{64,7... | collective-permute-start | bytes 14 | tf_op jit(solution)/shard_map/ppermute | solution.py:17
  17.9 1.9 gather_fusion
  19.8 2.0 fusion.49
  22.0 3.0 fusion.59
  25.0 6.9 %all-to-all-start.1 = ((bf16[32,2,8,128]{3,2,1,0:T(8,128)(2,1)}), bf16[32,2,8,128]{3,2,1,0:T(8,128)(2,1)S(1)}, u32[]{:S(2)}, u32[]{:S(2)}) async-start(bf16[32,2,8,128]{3,2,1,0:T(8,128)(2,1)} %fusion.59), calls=%async_computation.1 | async-start | bytes 262144 | tf_op jit(solution)/shard_map/all_to_all | solution.py:132
  33.2 3.4 fusion.56
  36.8 2.8 all-to-all-done.1
  39.6 4.6 all-to-all-start
  44.9 1.3 gather_fusion.2
  46.2 8.4 %all-to-all-done = bf16[32,2,8,288]{3,2,1,0:T(8,128)(2,1)S(1)} async-done(((bf16[32,2,8,288]{3,2,1,0:T(8,128)(2,1)}), bf16[32,2,8,288]{3,2,1,0:T(8,128)(2,1)S(1)}, u32[]{:S(2)}, u32[]{:S(2)}) %all-to-all-start) | async-done | bytes 294944 | tf_op jit(solution)/shard_map/all_to_all | solution.py:131
  57.0 1.3 pad_maximum_fusion.1
  59.7 1.9 collective-permute-start.1
  61.6 1.3 convolution_convert_fusion
  63.0 2.8 collective-permute-start
  65.7 1.5 bitcast_bitcast_fusion.1
  67.2 1.7 reshape.246
  69.0 3.0 reshape.250
  73.9 24.3 %while.21 = (s32[]{:T(128)}, f32[2,273,112]{2,1,0:T(8,128)S(1)}, f32[2,273]{0,1:T(8,128)S(1)}, s32[]{:T(128)}, bf16[2,2,256,112]{2,3,1,0:T(8,128)(2,1)}, /*index...) while((s32[]{:T(128)}, f32[2,273,112]{2,1,0:T(8,128)S(1)}, ...), condition=%wide.region_10.11_spmd, body=%wide.region_4.10_spmd.sunk | while | flops 1377437056 | bytes 23302216 | solution.py:188
  79.1 1.2 constant_dynamic-slice_fusion.7
  91.2 1.2 constant_dynamic-slice_fusion.7
  98.1 1.2 copy.102
  99.4 1.9 fusion.81
  101.3 2.0 add_convert_fusion
  103.3 1.1 constant_dynamic-slice_fusion.3
  104.5 14.5 %all_to_all.39 = bf16[32,2,8,224]{3,2,1,0:T(8,128)(2,1)S(1)} all-to-all(bf16[32,2,8,224]{3,2,1,0:T(8,128)(2,1)S(1)} %constant_dynamic-slice_fusion.3), channel_id=1, replica_groups=mesh['group'=32,'mp'=8] {'group'}, dimensions={0} | all-to-all | bytes 458752 | tf_op jit(solution)/shard_map/all_to_all | solution.py:130
  119.8 22.0 %reduce-scatter.2.cloned.1.call-done = bf16[512,224]{0,1:T(8,128)(2,1)} async-done(((bf16[512,1792]{0,1:T(8,128)(2,1)}), bf16[512,224]{0,1:T(8,128)(2,1)}) %reduce-scatter.2.cloned.1.call-update) | async-done | bytes 229392 | tf_op jit(solution)/shard_map/reduce_scatter | solution.py:212
  142.9 14.0 %all_to_all.40 = bf16[8,64,224]{2,1,0:T(8,128)(2,1)S(1)} all-to-all(bf16[8,64,224]{2,1,0:T(8,128)(2,1)S(1)} %bitcast.245), channel_id=1, replica_groups=mesh['group'=32,'mp'=8] {'mp'}, dimensions={0} | all-to-all | bytes 458752 | tf_op jit(solution)/shard_map/all_to_all | solution.py:216
  156.9 6.1 %stack.2 = bf16[256,16,1792]{2,1,0:T(8,128)(2,1)} broadcast(bf16[16,1792]{1,0:T(8,128)(2,1)S(1)} %copy-done.11), dimensions={1,2} | broadcast | bytes 14737408 | tf_op jit(solution)/shard_map/stack | solution.py:100
  163.1 13.4 %all-to-all-start.4 = ((bf16[256,16,1792]{2,1,0:T(8,128)(2,1)}), bf16[256,16,1792]{2,1,0:T(8,128)(2,1)}, u32[]{:S(2)}, u32[]{:S(2)}) async-start(bf16[256,16,1792]{2,1,0:T(8,128)(2,1)} %stack.2), calls=%async_computation.5 | async-start | bytes 29360128 | tf_op jit(solution)/shard_map/all_to_all | solution.py:100
  177.0 318.9 %all-to-all-done.4 = bf16[256,16,1792]{2,1,0:T(8,128)(2,1)} async-done(((bf16[256,16,1792]{2,1,0:T(8,128)(2,1)}), bf16[256,16,1792]{2,1,0:T(8,128)(2,1)}, u32[]{:S(2)}, u32[]{:S(2)}) %all-to-all-start.4) | async-done | bytes 14680096 | tf_op jit(solution)/shard_map/all_to_all | solution.py:100
  495.8 10.3 %convolution_reduce_fusion = f32[64]{0:T(128)} fusion(bf16[64,1792]{1,0:T(8,128)(2,1)S(1)} %all_to_all.32, bf16[4096,1792]{1,0:T(8,128)(2,1)} %bitcast.49), kind=kOutput, calls=%fused_computation.82 | convolution fusion | flops 939786176 | bytes 14909696 | tf_op jit(solution)/shard_map/rd,vd->rv/dot_general | solution.py:80
  (151 shorter events, 32.1 us)
Async XLA Ops:
  7.2 10.7 %copy-start = (bf16[512,1792]{1,0:T(8,128)(2,1)S(1)}, bf16[512,1792]{1,0:T(8,128)(2,1)}, u32[]{:S(2)}) copy-start(bf16[512,1792]{1,0:T(8,128)(2,1)} %param.13) | copy-start | bytes 5505028
  9.2 35.1 %collective-permute-start.2 = (bf16[1]{0:T(256)(128)(2,1)}, bf16[1]{0:T(256)(128)(2,1)}, u32[]{:S(2)}, u32[]{:S(2)}) collective-permute-start(bf16[1]{0:T(256)(128)(2,1)} %bitcast.30), channel_id=1, source_target_pairs={{0,8},{8,16},{16,24},{24,32},{32,40},{40,48},{48,56},{56,64},{64,7... | collective-permute-start | bytes 14 | tf_op jit(solution)/shard_map/ppermute | solution.py:17
  19.8 2.1 copy-start.16
  22.0 9.9 %copy-start.12 = (s32[512]{0:T(512)S(1)}, s32[512]{0:T(512)}, u32[]{:S(2)}) copy-start(s32[512]{0:T(512)} %param.20) | copy-start | bytes 6148
  22.0 10.6 %copy-start.13 = (s32[128]{0:T(128)S(1)}, s32[128]{0:T(128)}, u32[]{:S(2)}) copy-start(s32[128]{0:T(128)} %param.21) | copy-start | bytes 1540
  22.0 11.2 %copy-start.15 = (bf16[1792,288]{0,1:T(8,128)(2,1)S(1)}, bf16[1792,288]{0,1:T(8,128)(2,1)}, u32[]{:S(2)}) copy-start(bf16[1792,288]{0,1:T(8,128)(2,1)} %param.15) | copy-start | bytes 3096580
  25.0 14.6 %all-to-all-start.1 = ((bf16[32,2,8,128]{3,2,1,0:T(8,128)(2,1)}), bf16[32,2,8,128]{3,2,1,0:T(8,128)(2,1)S(1)}, u32[]{:S(2)}, u32[]{:S(2)}) async-start(bf16[32,2,8,128]{3,2,1,0:T(8,128)(2,1)} %fusion.59), calls=%async_computation.1 | async-start | bytes 262144 | tf_op jit(solution)/shard_map/all_to_all | solution.py:132
  33.2 3.5 copy-start.14
  39.6 14.9 %all-to-all-start = ((bf16[32,2,8,288]{3,2,1,0:T(8,128)(2,1)}), bf16[32,2,8,288]{3,2,1,0:T(8,128)(2,1)S(1)}, u32[]{:S(2)}, u32[]{:S(2)}) async-start(bf16[32,2,8,288]{3,2,1,0:T(8,128)(2,1)} %fusion.56), calls=%async_computation | async-start | bytes 786432 | tf_op jit(solution)/shard_map/all_to_all | solution.py:131
  44.2 97.6 %reduce-scatter.2.cloned.1.call-start = ((), (), s32[]{:S(2)}) async-start(), calls=%async_computation.6 | async-start | bytes 2064384 | tf_op jit(solution)/shard_map/reduce_scatter | solution.py:212
  55.8 0.8 copy-start.3
  55.9 2.4 copy-start.4
  59.7 12.3 %collective-permute-start.1 = (bf16[2,273]{0,1:T(8,128)(2,1)}, bf16[2,273]{0,1:T(8,128)(2,1)}, u32[]{:S(2)}, u32[]{:S(2)}) collective-permute-start(bf16[2,273]{0,1:T(8,128)(2,1)} %bitcast.141), channel_id=1, source_target_pairs={{0,8},{8,16},{16,24},{24,32},{32,40},{40,48},{48,56},{56,64},{64,7... | collective-permute-start | bytes 3284 | tf_op jit(solution)/shard_map/ppermute | solution.py:17
  63.0 6.0 %slice-start = ((f32[2,512,144]{1,2,0:T(8,128)}), f32[2,512,112]{1,2,0:T(8,128)S(1)}, s32[]{:S(2)}) async-start(f32[2,512,144]{1,2,0:T(8,128)} %copy-done.3), calls=%async_computation.7 | async-start | bytes 917504 | tf_op jit(solution)/shard_map/slice | solution.py:152
  63.0 9.9 %collective-permute-start = (bf16[2,273,112]{2,1,0:T(8,128)(2,1)}, bf16[2,273,112]{2,1,0:T(8,128)(2,1)}, u32[]{:S(2)}, u32[]{:S(2)}) collective-permute-start(bf16[2,273,112]{2,1,0:T(8,128)(2,1)} %convolution_convert_fusion), channel_id=1, source_target_pairs={{0,8},{8,16},{16,24},{24,32},{32,40},{40,48},{48,56},{56,64},{64,7... | collective-permute-start | bytes 366920 | tf_op jit(solution)/shard_map/ppermute | solution.py:17
  68.9 4.9 copy-start.5
  69.0 4.9 copy-start.10
  76.5 2.6 copy-start.1
  76.5 2.6 copy-start.2
  79.1 2.5 copy-start.8
  82.1 3.3 copy-start.9
  88.6 2.6 copy-start.1
  88.6 2.6 copy-start.2
  91.2 2.5 copy-start.8
  94.2 3.3 copy-start.9
  98.1 3.2 copy-start.17
  99.4 1.9 copy-start.6
  99.4 1.9 copy-start.7
  119.6 37.4 %copy-start.11 = (bf16[16,1792]{1,0:T(8,128)(2,1)S(1)}, bf16[16,1792]{1,0:T(8,128)(2,1)}, u32[]{:S(2)}) copy-start(bf16[16,1792]{1,0:T(8,128)(2,1)} %param.19) | copy-start | bytes 172036
  163.1 332.8 %all-to-all-start.4 = ((bf16[256,16,1792]{2,1,0:T(8,128)(2,1)}), bf16[256,16,1792]{2,1,0:T(8,128)(2,1)}, u32[]{:S(2)}, u32[]{:S(2)}) async-start(bf16[256,16,1792]{2,1,0:T(8,128)(2,1)} %stack.2), calls=%async_computation.5 | async-start | bytes 29360128 | tf_op jit(solution)/shard_map/all_to_all | solution.py:100
Sparse Core Ops, SparseCore 0:
  103.5 38.2 reduce-scatter.1
